TPU v7x, 32 devices: a whole 2x2x4 slice. The times are simulated.
32 devices in a mesh: shot: 16 (over z, y, core), rec: 2 (over x).
Axes of the slice: x: 2, y: 2, z: 4, core: 2. Of those that a mesh axis runs over, the one named last changes fastest.
Arguments:
- survey: float32 [2, 8, 2048, 2048], P(None, None, 'shot', 'rec'), may hold values from -1.5 to 1.5
- panel_index: int32 [2], replicated, may hold values from 0 to 31
Outputs:
- predicted: float32 [64, 2048, 2048], P(None, 'shot', 'rec')
Inputs may be any that keep to these rules, and one draw needn't show every extreme that they name: `panel_index`: panel numbers; one panel may come twice.
All inputs are finite; a program needn't handle non-finite values.
Results may differ from a plain program's by a relative error of at most 0.0001.
Values sent between devices are 32-bit elements; how exact they have to be, the bound alone decides.
A program may use at most 192 MiB of HBM per device.

v0:
```python
import functools
import math

import jax
import jax.numpy as jnp
import numpy as np
from jax import lax
from jax.experimental import pallas as pl
from jax.experimental.pallas import tpu as pltpu
from jax.sharding import PartitionSpec as P

FIRST_BIN = 8
TRACE_LEN = 400
SAMPLES = 64
PANEL = 64
STEPS = 2
PIECE_ROWS = 16


def from_root(array, axis, root):
    mine = lax.axis_index(axis) == root
    return lax.psum(jnp.where(mine, array, jnp.zeros_like(array)), axis)


def table(nfreq):
    bins = np.arange(nfreq) + FIRST_BIN
    moments = np.arange(SAMPLES)
    angle = (moments[:, None] * bins[None, :] % TRACE_LEN) * (2.0 * math.pi / TRACE_LEN)
    both = np.concatenate([np.cos(angle), -np.sin(angle)], axis=1)
    return (both / math.sqrt(nfreq)).astype(np.float32)


def kron_table(nfreq):
    flat = np.kron(table(nfreq), np.eye(8, dtype=np.float32))
    hi = flat.astype(jnp.bfloat16)
    lo = (flat - hi.astype(np.float32)).astype(jnp.bfloat16)
    return np.concatenate([hi, hi, lo], axis=1)


def broadcast_kernel(owner, depth, x_ref, o_ref, send_sem, recv_sem, whole_sem):
    del x_ref
    me = lax.axis_index("shot")
    z, y, c = me // 4, (me // 2) % 2, me % 2
    z0, y0, c0 = owner // 4, (owner // 2) % 2, owner % 2
    back = z0 + 1 if z0 < depth - 1 else z0 - 1
    count = o_ref.shape[1]
    is_owner = me == owner
    half = (c + c0) % 2
    main = (y + y0 + half) % 2 == 0
    root = (half == 1) & (z == z0) & (y == y0)
    extra = (half == 0) & (z == back) & (y != y0)
    up = main & (z >= z0) & (z < depth - 1)
    down = main & (z <= z0) & (z > 0)
    if back > z0:
        down = down | extra
    else:
        up = up | extra
    peer = me + 1 - 2 * c
    edges = [
        (0, up, me + 4),
        (1, down, me - 4),
        (2, (main & (z != z0)) | root, me + 2 - 4 * y),
        (3, jnp.logical_not(root), peer),
    ]

    def copy(at, send, arrive, target):
        return pltpu.make_async_remote_copy(
            src_ref=o_ref.at[at],
            dst_ref=o_ref.at[at],
            send_sem=send_sem.at[send],
            recv_sem=arrive,
            device_id={"shot": target},
            device_id_type=pl.DeviceIdType.MESH,
        )

    def forward(k):
        for slot, cond, target in edges:
            @pl.when(cond)
            def _():
                arrive = whole_sem if slot == 3 else recv_sem.at[k]
                copy((half, k), slot, arrive, target).start()

    def loop(body):
        def step(k, carry):
            body(k)
            return carry

        lax.fori_loop(0, count, step, 0)

    @pl.when(is_owner)
    def _():
        def step(k):
            copy((1, k), 4, recv_sem.at[k], peer).start()
            forward(k)

        loop(step)
        copy(1, 4, whole_sem, peer).wait_send()

    @pl.when(jnp.logical_not(is_owner))
    def _():
        def step(k):
            copy((half, k), 3, recv_sem.at[k], peer).wait_recv()
            forward(k)

        loop(step)
        copy(1 - half, 3, whole_sem, peer).wait_recv()

    for slot, cond, target in edges:
        @pl.when(cond)
        def _():
            copy(half, slot, whole_sem, target).wait_send()


def broadcast_rows(piece, owner, shots):
    shape = piece.shape
    count = shape[1] * shape[2] // PIECE_ROWS
    flat = piece.reshape(2, count, PIECE_ROWS, shape[3])

    def call(device):
        return pl.pallas_call(
            functools.partial(broadcast_kernel, device, shots // 4),
            out_shape=jax.ShapeDtypeStruct(flat.shape, flat.dtype),
            in_specs=[pl.BlockSpec(memory_space=pl.ANY)],
            out_specs=pl.BlockSpec(memory_space=pl.ANY),
            scratch_shapes=[
                pltpu.SemaphoreType.DMA((5,)),
                pltpu.SemaphoreType.DMA((count,)),
                pltpu.SemaphoreType.DMA,
            ],
            input_output_aliases={0: 0},
            compiler_params=pltpu.CompilerParams(has_side_effects=True),
            name="rows_from_%d" % device,
        )

    out = lax.switch(owner, [call(device) for device in range(shots)], flat)
    return out.reshape(shape)


def split(array):
    hi = array.astype(jnp.bfloat16)
    return hi, (array - hi.astype(jnp.float32)).astype(jnp.bfloat16)


def dot(left, right):
    return jnp.dot(left, right, preferred_element_type=jnp.float32)


def predict_kernel(
    own_ref, mine_ref, other_ref, row0_ref, row1_ref, table_ref, out_ref,
    left_hi, left_lo, freq_ref,
):
    nfreq = mine_ref.shape[1]
    rows = mine_ref.shape[2]
    tile = out_ref.shape[2]

    @pl.when(pl.program_id(0) == 0)
    def _():
        lane = lax.broadcasted_iota(jnp.int32, (rows, 2 * PANEL), 1)
        own = jnp.where(lane < PANEL, own_ref[0], own_ref[1]) == 1
        for f in range(nfreq):
            real = jnp.where(own, mine_ref[0, f], other_ref[0, f])
            imag = jnp.where(own, mine_ref[1, f], other_ref[1, f])
            top = jnp.concatenate([real, -imag], axis=1)
            low = jnp.concatenate([imag, real], axis=1)
            hi, lo = split(jnp.concatenate([top, low], axis=0))
            left_hi[f] = hi
            left_lo[f] = lo

    for f in range(nfreq):
        right = jnp.concatenate(
            [row0_ref[0, f], row1_ref[0, f], row0_ref[1, f], row1_ref[1, f]], axis=0
        )
        hi, lo = split(right)
        both = dot(left_hi[f], hi) + dot(left_lo[f], hi) + dot(left_hi[f], lo)
        freq_ref[f] = both[:rows]
        freq_ref[nfreq + f] = both[rows:]

    for g in range(rows // 8):
        part = freq_ref[:, 8 * g : 8 * g + 8, :].reshape(16 * nfreq, tile)
        hi, lo = split(part)
        done = dot(table_ref[...], jnp.concatenate([hi, lo, hi], axis=0))
        out_ref[:, 8 * g : 8 * g + 8, :] = done.reshape(SAMPLES, 8, tile)


def predict(own, mine, other, row0, row1):
    _, nfreq, rows, width = mine.shape
    cols = row0.shape[3]
    tile = min(256, cols)
    big = jnp.asarray(kron_table(nfreq))
    whole = pl.BlockSpec(mine.shape, lambda j: (0, 0, 0, 0))
    row_spec = pl.BlockSpec((2, nfreq, PANEL, tile), lambda j: (0, 0, 0, j))
    return pl.pallas_call(
        predict_kernel,
        grid=(cols // tile,),
        out_shape=jax.ShapeDtypeStruct((SAMPLES, rows, cols), jnp.float32),
        in_specs=[
            pl.BlockSpec(memory_space=pltpu.SMEM),
            whole,
            whole,
            row_spec,
            row_spec,
            pl.BlockSpec(big.shape, lambda j: (0, 0)),
        ],
        out_specs=pl.BlockSpec((SAMPLES, rows, tile), lambda j: (0, 0, j)),
        scratch_shapes=[
            pltpu.VMEM((nfreq, 2 * rows, 4 * PANEL), jnp.bfloat16),
            pltpu.VMEM((nfreq, 2 * rows, 4 * PANEL), jnp.bfloat16),
            pltpu.VMEM((2 * nfreq, rows, tile), jnp.float32),
        ],
        compiler_params=pltpu.CompilerParams(vmem_limit_bytes=48 << 20),
        name="predict",
    )(own, mine, other, row0, row1, big)


def fetch_rows(source, start, shot_rows):
    length = min(shot_rows, PANEL)
    pieces = []
    for index_piece in range(PANEL // length):
        first = start + index_piece * length
        owner = first // shot_rows
        offset = first % shot_rows
        piece = lax.dynamic_slice_in_dim(source, offset, length, 2)
        pieces.append(from_root(piece, "shot", owner))
    return jnp.concatenate(pieces, axis=2)


def shards(tree, shots, recs, survey, panel_index):
    shot_rows = survey.shape[2]
    rec_cols = survey.shape[3]
    starts = [panel_index[step] * PANEL for step in range(STEPS)]
    columns = [
        lax.dynamic_slice_in_dim(survey, start % rec_cols, PANEL, 3) for start in starts
    ]
    owners = jnp.stack([start // rec_cols for start in starts])
    me = lax.axis_index("rec")
    mine = jnp.concatenate(columns, axis=3)
    if tree:
        other = lax.ppermute(mine, "rec", [(0, 1), (1, 0)])
        own = (owners == me).astype(jnp.int32)
        rows = []
        for start in starts:
            piece = lax.dynamic_slice_in_dim(survey, start % shot_rows, PANEL, 2)
            rows.append(broadcast_rows(piece, start // shot_rows, shots))
    else:
        wanted = jnp.repeat(owners == me, PANEL, total_repeat_length=STEPS * PANEL)
        mine = lax.psum(jnp.where(wanted, mine, 0.0), "rec")
        other = mine
        own = jnp.ones((STEPS,), jnp.int32)
        rows = [fetch_rows(survey, start, shot_rows) for start in starts]
    return predict(own, mine, other, rows[0], rows[1])


def solution(mesh):
    shots, recs = mesh.shape["shot"], mesh.shape["rec"]
    tree = (shots, recs) == (16, 2)
    return jax.shard_map(
        functools.partial(shards, tree, shots, recs),
        mesh=mesh,
        in_specs=(P(None, None, "shot", "rec"), P()),
        out_specs=P(None, "shot", "rec"),
        check_vma=False,
    )
```

profile of v0, /device:TPU:5, one launch (start us, length us, event | category | flops | bytes accessed | tf_op | source)
XLA Modules:
  0.0 122.1 jit_solution(4350998210348387656)
XLA Ops:
  0.0 1.4 %fusion = (s32[1]{0:T(128)}, s32[1]{0:T(128)}) fusion(s32[2]{0:T(128)} %param.36), kind=kLoop, calls=%fused_computation.36 | loop fusion | bytes 16 | tf_op jit(solution)/shard_map/slice | solution.py:230
  2.8 2.9 %constant_dynamic-slice_fusion.33 = (f32[2,8,128,64]{3,2,1,0:T(8,128)S(1)}, f32[2,8,128,64]{3,2,1,0:T(8,128)S(1)}) fusion(f32[2,8,128,1024]{3,2,1,0:T(8,128)} %param.35, s32[]{:T(128)S(6)} %select_n.171, s32[]{:T(128)S(6)} %select_n.173), kind=kLoop, calls=%fused_computation.35 | loop fusion | bytes 2097160 | tf_op jit(solution)/shard_map/dynamic_slice | solution.py:232
  5.6 1.4 %pad_maximum_fusion.mine_ref = f32[2,8,128,128]{3,2,1,0:T(8,128)} fusion(f32[2,8,128,64]{3,2,1,0:T(8,128)S(1)} %get-tuple-element.970, f32[2,8,128,64]{3,2,1,0:T(8,128)S(1)} %get-tuple-element.969), kind=kLoop, calls=%fused_computation.32 | loop fusion | flops 262144 | bytes 2097152 | tf_op jit(solution)/shard_map/concatenate | solution.py:236
  7.0 1.2 collective-permute-start
  8.2 48.4 %conditional.3 = (f32[2,8,64,1024]{3,2,1,0:T(8,128)}) conditional(s32[]{:T(128)} %clamp.7, (s32[]{:T(128)}, f32[2,8,128,1024]{3,2,1,0:T(8,128)}) %tuple.230, (s32[]{:T(128)}, f32[2,8,128,1024]{3,2,1,0:T(8,128)}) %tuple.230, (s32[]{:T(128)}, f32[2,8,128,1024]{3,2,1,0:T(8,128)}) %tuple.230, (s32[]{:T(128)}, ...), branch_computations={%region_16.17_spmd, %region_17.18_spmd, %region_18.19_spmd, %regio... | conditional | flops 3 | bytes 8388654 | solution.py:135
  8.2 5.2 %constant_dynamic-slice_fusion.26 = f32[2,8,64,1024]{3,2,1,0:T(8,128)} fusion(f32[2,8,128,1024]{3,2,1,0:T(8,128)} %get-tuple-element.957, s32[]{:T(128)S(6)} %select_n.152), kind=kLoop, calls=%fused_computation.26 | loop fusion | bytes 8388612 | tf_op jit(solution)/shard_map/dynamic_slice | solution.py:242
  13.4 43.1 %rows_from_10.5 = f32[2,32,16,1024]{3,2,1,0:T(8,128)} custom-call(f32[2,32,16,1024]{3,2,1,0:T(8,128)} %bitcast.88), custom_call_target="tpu_custom_call", output_to_operand_aliasing={{}: (0, {})} | custom-call | tf_op jit(solution)/shard_map/cond/branch_10_fun/rows_from_10/pallas_call | solution.py:135
  56.7 0.0 copy-start
  56.7 45.8 %conditional.2 = (f32[2,8,64,1024]{3,2,1,0:T(8,128)}) conditional(s32[]{:T(128)} %clamp.6, (s32[]{:T(128)}, f32[2,8,128,1024]{3,2,1,0:T(8,128)}) %tuple.229, (s32[]{:T(128)}, f32[2,8,128,1024]{3,2,1,0:T(8,128)}) %tuple.229, (s32[]{:T(128)}, f32[2,8,128,1024]{3,2,1,0:T(8,128)}) %tuple.229, (s32[]{:T(128)}, ...), branch_computations={%region_0.1_spmd, %region_1.2_spmd, %region_2.3_spmd, %region_3.4_... | conditional | flops 3 | bytes 8388654 | solution.py:135
  56.7 5.2 %constant_dynamic-slice_fusion.10 = f32[2,8,64,1024]{3,2,1,0:T(8,128)} fusion(f32[2,8,128,1024]{3,2,1,0:T(8,128)} %get-tuple-element.925, s32[]{:T(128)S(6)} %select_n.136), kind=kLoop, calls=%fused_computation.10 | loop fusion | bytes 8388612 | tf_op jit(solution)/shard_map/dynamic_slice | solution.py:242
  61.9 40.4 %rows_from_10.4 = f32[2,32,16,1024]{3,2,1,0:T(8,128)} custom-call(f32[2,32,16,1024]{3,2,1,0:T(8,128)} %bitcast.120), custom_call_target="tpu_custom_call", output_to_operand_aliasing={{}: (0, {})} | custom-call | tf_op jit(solution)/shard_map/cond/branch_10_fun/rows_from_10/pallas_call | solution.py:135
  102.5 0.1 compare_convert_fusion.own_ref
  102.6 0.0 collective-permute-done.other_ref
  102.6 0.0 copy-done
  102.6 19.5 %predict.1 = f32[64,128,1024]{2,1,0:T(8,128)} custom-call(s32[2]{0:T(128)S(1)} %compare_convert_fusion.own_ref, f32[2,8,128,128]{3,2,1,0:T(8,128)} %pad_maximum_fusion.mine_ref, f32[2,8,128,128]{3,2,1,0:T(8,128)} %collective-permute-done.other_ref, f32[2,8,64,1024]{3,2,1,0:T(8,128)} %get-tuple-element.973.row0_ref, ...), custom_call_target="tpu_custom_call" | custom-call | tf_op jit(solution)/shard_map/predict/pallas_call | solution.py:192
Async XLA Ops:
  7.0 95.6 %collective-permute-start = (f32[2,8,128,128]{3,2,1,0:T(8,128)}, f32[2,8,128,128]{3,2,1,0:T(8,128)}, u32[]{:S(2)}, u32[]{:S(2)}) collective-permute-start(f32[2,8,128,128]{3,2,1,0:T(8,128)} %pad_maximum_fusion.mine_ref), channel_id=1, source_target_pairs={{0,1},{1,0},{2,3},{3,2},{4,5},{5,4},{6,7},{7,6},{8,9},{9,8},{10,11... | collective-permute-start | bytes 3145736 | tf_op jit(solution)/shard_map/ppermute | solution.py:238
  56.7 45.9 %copy-start = (bf16[512,384]{1,0:T(8,128)(2,1)S(1)}, bf16[512,384]{1,0:T(8,128)(2,1)}, u32[]{:S(2)}) copy-start(bf16[512,384]{1,0:T(8,128)(2,1)} %constant.240.clone.table_ref) | copy-start | bytes 1179652
where the time goes:
time: 122 us
  Pallas kernels  103 us (84%)
  local copies, waits for them, and re-layouts  14.6 us (12%)
  other arithmetic  1.47 us (1%)
  between operations  1.41 us (1%)
    pallas_call x2, Pallas kernels, broadcast_rows(): out = lax.switch(owner, [call(device) for device in range(shots)], flat)  83.5 us
    pallas_call x1, Pallas kernels, predict(): pl.pallas_call(predict_kernel, grid=(cols // tile,), out_shape=jax.ShapeD...  19.5 us
    dynamic_slice x2, local copies, waits for them, and re-layouts, shards(): piece = lax.dynamic_slice_in_dim(survey, start % shot_rows, PANEL, 2)  10.3 us
    dynamic_slice x1, local copies, waits for them, and re-layouts, shards(): lax.dynamic_slice_in_dim(survey, start % rec_cols, PANEL, 3)  2.85 us
  transfers between devices with their start and end apart: 1, of which 0 were waited for; matrix products, arithmetic and copies ran while one was open for 9% of the time, Pallas kernels for 68%

commit v1 on v0

--- a/solution.py
+++ b/solution.py
@@ -22,19 +22,22 @@
     return lax.psum(jnp.where(mine, array, jnp.zeros_like(array)), axis)
 
 
-def table(nfreq):
+def middle(f):
+    angle = 2.0 * math.pi * (f + FIRST_BIN) * (0.5 * (SAMPLES - 1)) / TRACE_LEN
+    return math.cos(angle), math.sin(angle)
+
+
+def kron_tables(nfreq):
+    moments = np.arange(SAMPLES // 2) + 0.5
     bins = np.arange(nfreq) + FIRST_BIN
-    moments = np.arange(SAMPLES)
-    angle = (moments[:, None] * bins[None, :] % TRACE_LEN) * (2.0 * math.pi / TRACE_LEN)
-    both = np.concatenate([np.cos(angle), -np.sin(angle)], axis=1)
-    return (both / math.sqrt(nfreq)).astype(np.float32)
-
-
-def kron_table(nfreq):
-    flat = np.kron(table(nfreq), np.eye(8, dtype=np.float32))
-    hi = flat.astype(jnp.bfloat16)
-    lo = (flat - hi.astype(np.float32)).astype(jnp.bfloat16)
-    return np.concatenate([hi, hi, lo], axis=1)
+    angle = moments[:, None] * bins[None, :] * (2.0 * math.pi / TRACE_LEN)
+    parts = []
+    for wave in (np.cos(angle), np.sin(angle)):
+        flat = np.kron(wave / math.sqrt(nfreq), np.eye(8)).astype(np.float32)
+        hi = flat.astype(jnp.bfloat16)
+        lo = (flat - hi.astype(np.float32)).astype(jnp.bfloat16)
+        parts.append(np.concatenate([hi, hi, lo], axis=1))
+    return np.stack(parts)
 
 
 def broadcast_kernel(owner, depth, x_ref, o_ref, send_sem, recv_sem, whole_sem):
@@ -160,6 +163,8 @@
         for f in range(nfreq):
             real = jnp.where(own, mine_ref[0, f], other_ref[0, f])
             imag = jnp.where(own, mine_ref[1, f], other_ref[1, f])
+            cos, sin = middle(f)
+            real, imag = real * cos - imag * sin, real * sin + imag * cos
             top = jnp.concatenate([real, -imag], axis=1)
             low = jnp.concatenate([imag, real], axis=1)
             hi, lo = split(jnp.concatenate([top, low], axis=0))
@@ -175,18 +180,26 @@
         freq_ref[f] = both[:rows]
         freq_ref[nfreq + f] = both[rows:]
 
+    half = SAMPLES // 2
     for g in range(rows // 8):
-        part = freq_ref[:, 8 * g : 8 * g + 8, :].reshape(16 * nfreq, tile)
-        hi, lo = split(part)
-        done = dot(table_ref[...], jnp.concatenate([hi, lo, hi], axis=0))
-        out_ref[:, 8 * g : 8 * g + 8, :] = done.reshape(SAMPLES, 8, tile)
+        at = slice(8 * g, 8 * g + 8)
+        waves = []
+        for i in (0, 1):
+            part = freq_ref[i * nfreq : (i + 1) * nfreq, at, :].reshape(8 * nfreq, tile)
+            hi, lo = split(part)
+            waves.append(dot(table_ref[i], jnp.concatenate([hi, lo, hi], axis=0)))
+        even, odd = waves
+        out_ref[half:, at, :] = (even - odd).reshape(half, 8, tile)
+        early = even + odd
+        for j in range(half):
+            out_ref[half - 1 - j, at, :] = early[8 * j : 8 * j + 8]
 
 
 def predict(own, mine, other, row0, row1):
     _, nfreq, rows, width = mine.shape
     cols = row0.shape[3]
     tile = min(256, cols)
-    big = jnp.asarray(kron_table(nfreq))
+    big = jnp.asarray(kron_tables(nfreq))
     whole = pl.BlockSpec(mine.shape, lambda j: (0, 0, 0, 0))
     row_spec = pl.BlockSpec((2, nfreq, PANEL, tile), lambda j: (0, 0, 0, j))
     return pl.pallas_call(
@@ -199,7 +212,7 @@
             whole,
             row_spec,
             row_spec,
-            pl.BlockSpec(big.shape, lambda j: (0, 0)),
+            pl.BlockSpec(big.shape, lambda j: (0, 0, 0)),
         ],
         out_specs=pl.BlockSpec((SAMPLES, rows, tile), lambda j: (0, 0, j)),
         scratch_shapes=[

time: 122 us -> 121 us (level)
  the two profiles are of different devices: /device:TPU:5 before, /device:TPU:25 now
where the time goes in v1:
time: 121 us; the launch traced here: 120 us
  Pallas kernels  101 us (83%)
  local copies, waits for them, and re-layouts  14.7 us (12%)
  other arithmetic  1.47 us (1%)
  between operations  1.41 us (1%)
  starting transfers between devices  1.21 us (1%)
    pallas_call x2, Pallas kernels, broadcast_rows(): out = lax.switch(owner, [call(device) for device in range(shots)], flat)  83.5 us
    pallas_call x1, Pallas kernels, predict(): pl.pallas_call(predict_kernel, grid=(cols // tile,), out_shape=jax.ShapeD...  17.3 us
    dynamic_slice x2, local copies, waits for them, and re-layouts, shards(): piece = lax.dynamic_slice_in_dim(survey, start % shot_rows, PANEL, 2)  10.5 us
    dynamic_slice x1, local copies, waits for them, and re-layouts, shards(): lax.dynamic_slice_in_dim(survey, start % rec_cols, PANEL, 3)  2.85 us
  transfers between devices with their start and end apart: 1, of which 0 were waited for; matrix products, arithmetic and copies ran while one was open for 9% of the time, Pallas kernels for 70%

profile of v1, /device:TPU:25, one launch (start us, length us, event | category | flops | bytes accessed | tf_op | source)
XLA Modules:
  0.0 120.1 jit_solution(1375871041121525795)
XLA Ops:
  0.0 1.4 %fusion = (s32[1]{0:T(128)}, s32[1]{0:T(128)}) fusion(s32[2]{0:T(128)} %param.36), kind=kLoop, calls=%fused_computation.36 | loop fusion | bytes 16 | tf_op jit(solution)/shard_map/slice | solution.py:243
  2.8 2.9 %constant_dynamic-slice_fusion.33 = (f32[2,8,128,64]{3,2,1,0:T(8,128)S(1)}, f32[2,8,128,64]{3,2,1,0:T(8,128)S(1)}) fusion(f32[2,8,128,1024]{3,2,1,0:T(8,128)} %param.35, s32[]{:T(128)S(6)} %select_n.171, s32[]{:T(128)S(6)} %select_n.173), kind=kLoop, calls=%fused_computation.35 | loop fusion | bytes 2097160 | tf_op jit(solution)/shard_map/dynamic_slice | solution.py:245
  5.6 1.4 %pad_maximum_fusion.mine_ref = f32[2,8,128,128]{3,2,1,0:T(8,128)} fusion(f32[2,8,128,64]{3,2,1,0:T(8,128)S(1)} %get-tuple-element.970, f32[2,8,128,64]{3,2,1,0:T(8,128)S(1)} %get-tuple-element.969), kind=kLoop, calls=%fused_computation.32 | loop fusion | flops 262144 | bytes 2097152 | tf_op jit(solution)/shard_map/concatenate | solution.py:249
  7.0 1.2 %collective-permute-start = (f32[2,8,128,128]{3,2,1,0:T(8,128)}, f32[2,8,128,128]{3,2,1,0:T(8,128)}, u32[]{:S(2)}, u32[]{:S(2)}) collective-permute-start(f32[2,8,128,128]{3,2,1,0:T(8,128)} %pad_maximum_fusion.mine_ref), channel_id=1, source_target_pairs={{0,1},{1,0},{2,3},{3,2},{4,5},{5,4},{6,7},{7,6},{8,9},{9,8},{10,11... | collective-permute-start | bytes 3145736 | tf_op jit(solution)/shard_map/ppermute | solution.py:251
  8.2 44.5 %conditional.3 = (f32[2,8,64,1024]{3,2,1,0:T(8,128)}) conditional(s32[]{:T(128)} %clamp.7, (s32[]{:T(128)}, f32[2,8,128,1024]{3,2,1,0:T(8,128)}) %tuple.230, (s32[]{:T(128)}, f32[2,8,128,1024]{3,2,1,0:T(8,128)}) %tuple.230, (s32[]{:T(128)}, f32[2,8,128,1024]{3,2,1,0:T(8,128)}) %tuple.230, (s32[]{:T(128)}, ...), branch_computations={%region_16.17_spmd, %region_17.18_spmd, %region_18.19_spmd, %regio... | conditional | flops 3 | bytes 8388654 | solution.py:138
  8.2 5.2 %constant_dynamic-slice_fusion.22 = f32[2,8,64,1024]{3,2,1,0:T(8,128)} fusion(f32[2,8,128,1024]{3,2,1,0:T(8,128)} %get-tuple-element.949, s32[]{:T(128)S(6)} %select_n.148), kind=kLoop, calls=%fused_computation.22 | loop fusion | bytes 8388612 | tf_op jit(solution)/shard_map/dynamic_slice | solution.py:255
  13.4 39.2 %rows_from_6.5 = f32[2,32,16,1024]{3,2,1,0:T(8,128)} custom-call(f32[2,32,16,1024]{3,2,1,0:T(8,128)} %bitcast.80), custom_call_target="tpu_custom_call", output_to_operand_aliasing={{}: (0, {})} | custom-call | tf_op jit(solution)/shard_map/cond/branch_6_fun/rows_from_6/pallas_call | solution.py:138
  52.8 0.0 copy-start
  52.8 49.9 %conditional.2 = (f32[2,8,64,1024]{3,2,1,0:T(8,128)}) conditional(s32[]{:T(128)} %clamp.6, (s32[]{:T(128)}, f32[2,8,128,1024]{3,2,1,0:T(8,128)}) %tuple.229, (s32[]{:T(128)}, f32[2,8,128,1024]{3,2,1,0:T(8,128)}) %tuple.229, (s32[]{:T(128)}, f32[2,8,128,1024]{3,2,1,0:T(8,128)}) %tuple.229, (s32[]{:T(128)}, ...), branch_computations={%region_0.1_spmd, %region_1.2_spmd, %region_2.3_spmd, %region_3.4_... | conditional | flops 3 | bytes 8388654 | solution.py:138
  52.8 5.3 %constant_dynamic-slice_fusion.2 = f32[2,8,64,1024]{3,2,1,0:T(8,128)} fusion(f32[2,8,128,1024]{3,2,1,0:T(8,128)} %get-tuple-element.909, s32[]{:T(128)S(6)} %select_n.128), kind=kLoop, calls=%fused_computation.2 | loop fusion | bytes 8388612 | tf_op jit(solution)/shard_map/dynamic_slice | solution.py:255
  58.1 44.3 %rows_from_2.4 = f32[2,32,16,1024]{3,2,1,0:T(8,128)} custom-call(f32[2,32,16,1024]{3,2,1,0:T(8,128)} %bitcast.104), custom_call_target="tpu_custom_call", output_to_operand_aliasing={{}: (0, {})} | custom-call | tf_op jit(solution)/shard_map/cond/branch_2_fun/rows_from_2/pallas_call | solution.py:138
  102.7 0.1 compare_convert_fusion.own_ref
  102.8 0.0 collective-permute-done.other_ref
  102.8 0.0 copy-done
  102.8 17.3 %predict.1 = f32[64,128,1024]{2,1,0:T(8,128)} custom-call(s32[2]{0:T(128)S(1)} %compare_convert_fusion.own_ref, f32[2,8,128,128]{3,2,1,0:T(8,128)} %pad_maximum_fusion.mine_ref, f32[2,8,128,128]{3,2,1,0:T(8,128)} %collective-permute-done.other_ref, f32[2,8,64,1024]{3,2,1,0:T(8,128)} %get-tuple-element.973.row0_ref, ...), custom_call_target="tpu_custom_call" | custom-call | tf_op jit(solution)/shard_map/predict/pallas_call | solution.py:205
Async XLA Ops:
  7.0 95.8 %collective-permute-start = (f32[2,8,128,128]{3,2,1,0:T(8,128)}, f32[2,8,128,128]{3,2,1,0:T(8,128)}, u32[]{:S(2)}, u32[]{:S(2)}) collective-permute-start(f32[2,8,128,128]{3,2,1,0:T(8,128)} %pad_maximum_fusion.mine_ref), channel_id=1, source_target_pairs={{0,1},{1,0},{2,3},{3,2},{4,5},{5,4},{6,7},{7,6},{8,9},{9,8},{10,11... | collective-permute-start | bytes 3145736 | tf_op jit(solution)/shard_map/ppermute | solution.py:251
  52.8 50.0 %copy-start = (bf16[2,256,192]{2,1,0:T(8,128)(2,1)S(1)}, bf16[2,256,192]{2,1,0:T(8,128)(2,1)}, u32[]{:S(2)}) copy-start(bf16[2,256,192]{2,1,0:T(8,128)(2,1)} %constant.240.clone.table_ref) | copy-start | bytes 589828
